TPU v7x, 32 devices: a whole 2x2x4 slice. The times are simulated.
32 devices in a mesh: groups: 2 (over x), branch: 2 (over core), sub: 8 (over z, y).
Axes of the slice: x: 2, y: 2, z: 4, core: 2. Of those that a mesh axis runs over, the one named last changes fastest.
Arguments:
- dispatch: float32 [128, 168, 2048], P(('groups', 'branch', 'sub')), parts along dimension 0, may hold values from 0 to 3
- multiplier: float32 [128, 48, 2048], P(('groups', 'branch', 'sub')), parts along dimension 0, may hold values from -3 to 3
- node_of: int32 [128], P(('groups', 'branch', 'sub')), parts along dimension 0, may hold values from 0 to 7, as said below
- prob_weight: int32 [128], P(('groups', 'branch', 'sub')), parts along dimension 0, may hold values from 1 to 16
- commitment: int32 [128, 168, 2048], P(('groups', 'branch', 'sub')), parts along dimension 0, may hold values 0 or 1
- zone_of: int32 [2048], replicated, may hold values from 0 to 31
- capacity: float32 [2048], replicated, may hold values from 0.5 to 4
- linear_cost: float32 [2048], replicated, may hold values from -0.5 to 1
- quad_cost: float32 [2048], replicated, may hold values from 0.5 to 2
- demand: float32 [128, 168, 32], P(('groups', 'branch', 'sub')), parts along dimension 0, may hold values from 19 to 64
Outputs:
- new_dispatch: float32 [128, 168, 2048], P(('groups', 'branch', 'sub')), parts along dimension 0
- new_multiplier: float32 [128, 48, 2048], P(('groups', 'branch', 'sub')), parts along dimension 0
- next_average: float32 [128, 48, 2048], P(('groups', 'branch', 'sub')), parts along dimension 0
- deviation: float32 [2], P('groups'), parts along dimension 0
There are 2 independent parts, one for each index of `groups`. A program takes and returns all parts, laid end to end along the dimension named above; an argument that names none is the same for every part. Nothing has to cross between parts.
Inputs may be any that keep to these rules, and one draw needn't show every extreme that they name: `node_of`: within each aligned block of 32 scenarios (one day-one branch), every node number holds exactly 4 scenarios.
All inputs are finite; a program needn't handle non-finite values. No bound on the sum of `commitment` on one device may be relied on, other than what follows from the above.
Results may differ from a plain program's by a relative error of at most 0.0001.
Values sent between devices are 32-bit elements; how exact they have to be, the bound alone decides.
A program may use at most 128 MiB of HBM per device.

v0:
```python
import jax
import jax.numpy as jnp
from jax import lax
from jax.sharding import PartitionSpec as P

DAY = 24
NODES_BR = 8
STEPS = 3
rho_value = 1.0
step_size = 0.3


def average(early_part, prob_weight, node_of, riding):
    weighting = prob_weight.astype(jnp.float32)
    scen_local = early_part.shape[0]
    gens = early_part.shape[2]
    member = (node_of[None, :] == jnp.arange(NODES_BR, dtype=jnp.int32)[:, None]).astype(
        jnp.float32
    )
    weighted = member * weighting[None, :]
    day_one = jnp.einsum(
        "s,stg->tg", weighting, early_part[:, :DAY], precision=lax.Precision.HIGHEST
    )
    weight_sum = jnp.sum(weighting)[None]
    day_two = jnp.einsum(
        "ks,stg->ktg", weighted, early_part[:, DAY:], precision=lax.Precision.HIGHEST
    )
    node_weight = jnp.sum(weighted, axis=1)
    day_two, node_weight = lax.psum((day_two, node_weight), "sub")
    day_one, weight_sum, riding = lax.psum((day_one, weight_sum, riding), ("branch", "sub"))
    root_mean = day_one / weight_sum[0]
    node_mean = day_two / node_weight[:, None, None]
    assigned = jnp.einsum("ks,ktg->stg", member, node_mean, precision=lax.Precision.HIGHEST)
    spread_root = jnp.broadcast_to(root_mean[None], (scen_local, DAY, gens))
    return (jnp.concatenate([spread_root, assigned], axis=1), weight_sum, riding)


def shards(
    dispatch,
    multiplier,
    node_of,
    prob_weight,
    commitment,
    zone_of,
    capacity,
    linear_cost,
    quad_cost,
    demand,
):
    section_hours = multiplier.shape[1]
    gens = zone_of.shape[0]
    zones_count = demand.shape[2]
    weighting = prob_weight.astype(jnp.float32)
    nothing = jnp.zeros((1,), jnp.float32)
    averages, weight_sum, unused = average(
        dispatch[:, :section_hours], prob_weight, node_of, nothing
    )
    spread_gap = dispatch[:, :section_hours] - averages
    local_spread = jnp.sum(weighting[:, None, None] * spread_gap * spread_gap)[None]
    dev_total = lax.psum(local_spread, ("branch", "sub"))
    new_multiplier = multiplier + rho_value * spread_gap
    zone_table = (zone_of[:, None] == jnp.arange(zones_count, dtype=jnp.int32)[None, :]).astype(
        jnp.float32
    )
    ceiling = capacity[None, None, :] * commitment.astype(jnp.float32)
    balance = zones_count / gens
    current = dispatch
    for sweep in range(STEPS):
        zone_sum = jnp.einsum("stg,gz->stz", current, zone_table, precision=lax.Precision.HIGHEST)
        mismatch = zone_sum - demand
        feedback = jnp.einsum("stz,gz->stg", mismatch, zone_table, precision=lax.Precision.HIGHEST)
        gradient = linear_cost + quad_cost * current + balance * feedback
        hedged = (
            gradient[:, :section_hours]
            + new_multiplier
            + rho_value * (current[:, :section_hours] - averages)
        )
        gradient = jnp.concatenate([hedged, gradient[:, section_hours:]], axis=1)
        current = jnp.clip(current - step_size * gradient, 0.0, ceiling)
    next_average, unused_sum, carried = average(
        current[:, :section_hours], prob_weight, node_of, nothing
    )
    deviation = dev_total / (weight_sum * section_hours * gens)
    return (current, new_multiplier, next_average, deviation)


def solution(mesh):
    in_specs = (
        P(("groups", "branch", "sub"), None, None),
        P(("groups", "branch", "sub"), None, None),
        P(("groups", "branch", "sub")),
        P(("groups", "branch", "sub")),
        P(("groups", "branch", "sub"), None, None),
        P(),
        P(),
        P(),
        P(),
        P(("groups", "branch", "sub"), None, None),
    )
    out_specs = (
        P(("groups", "branch", "sub"), None, None),
        P(("groups", "branch", "sub"), None, None),
        P(("groups", "branch", "sub"), None, None),
        P("groups"),
    )
    return jax.shard_map(shards, mesh=mesh, in_specs=in_specs, out_specs=out_specs, check_vma=False)
```

profile of v0, /device:TPU:0, one launch (start us, length us, event | category | flops | bytes accessed | tf_op | source)
XLA Modules:
  0.0 428.4 jit_solution(12756518674870253161)
XLA Ops:
  8.8 2.5 fusion.25
  12.7 4.0 fusion.23
  17.5 35.9 %psum.56 = f32[1]{0:T(128)} all-reduce(f32[1]{0:T(128)} %bitcast.4), channel_id=1, replica_groups=mesh['groups'=2,'branch'=2,'sub'=8] {'branch','sub'}, use_global_device_ids=true, to_apply=%region_2.0 | all-reduce | flops 1 | bytes 8 | tf_op jit(solution)/shard_map/psum | solution.py:30
  53.4 17.6 %psum.58 = f32[8]{0:T(128)S(1)} all-reduce(f32[8]{0:T(128)S(1)} %select_reduce_fusion), channel_id=1, replica_groups=mesh['groups'=2,'branch'=2,'sub'=8] {'sub'}, use_global_device_ids=true, to_apply=%region_5.0 | all-reduce | flops 8 | bytes 64 | tf_op jit(solution)/shard_map/psum | solution.py:29
  71.1 5.7 %fusion.18 = f32[4,168,32]{1,2,0:T(8,128)S(1)} fusion(f32[4,168,32]{1,2,0:T(8,128)S(1)} %copy-done.6, f32[4,168,2048]{2,1,0:T(8,128)} %param.10, s32[2048]{0:T(1024)S(1)} %copy-done.7), kind=kOutput, calls=%fused_computation.36 | convolution fusion | flops 528569344 | bytes 5685248 | tf_op jit(solution)/shard_map/stg,gz->stz/dot_general | solution.py:69
  76.8 3.0 multiply_add_fusion.2
  79.8 2.4 copy-done.1
  82.2 22.3 %all-reduce.5.cloned.1.call-done = f32[24,2048]{1,0:T(8,128)} async-done(((f32[24,2048]{1,0:T(8,128)}), f32[24,2048]{1,0:T(8,128)}) %all-reduce.5.cloned.1.call-update) | async-done | bytes 196624 | tf_op jit(solution)/shard_map/psum | solution.py:30
  106.1 90.5 %all-reduce.7.cloned.1.call-done = f32[8,24,2048]{2,0,1:T(8,128)} async-done(((f32[8,24,2048]{2,0,1:T(8,128)}), f32[8,24,2048]{2,0,1:T(8,128)}) %all-reduce.7.cloned.1.call-update) | async-done | bytes 1572880 | tf_op jit(solution)/shard_map/psum | solution.py:29
  196.5 2.5 fusion.16
  199.7 2.9 fusion.12
  204.0 4.0 fusion.2
  208.0 3.0 convolution_subtract_fusion.1
  211.0 3.0 multiply_add_fusion.1
  216.7 2.9 fusion.5
  219.6 3.0 convolution_subtract_fusion
  222.6 3.0 multiply_add_fusion
  226.4 2.6 fusion.8
  229.1 2.4 copy-done.4
  234.3 3.3 fusion.19
  238.3 32.6 %psum.61 = f32[1]{0:T(128)} all-reduce(f32[1]{0:T(128)} %bitcast.10), channel_id=1, replica_groups=mesh['groups'=2,'branch'=2,'sub'=8] {'branch','sub'}, use_global_device_ids=true, to_apply=%region_9.10 | all-reduce | flops 1 | bytes 8 | tf_op jit(solution)/shard_map/psum | solution.py:60
  271.5 52.0 %all-reduce.9.cloned.1.call-done = f32[24,2048]{1,0:T(8,128)} async-done(((f32[24,2048]{1,0:T(8,128)}), f32[24,2048]{1,0:T(8,128)}) %all-reduce.9.cloned.1.call-update) | async-done | bytes 196624 | tf_op jit(solution)/shard_map/psum | solution.py:30
  325.1 90.3 %all-reduce.11.cloned.1.call-done = f32[8,24,2048]{2,0,1:T(8,128)} async-done(((f32[8,24,2048]{2,0,1:T(8,128)}), f32[8,24,2048]{2,0,1:T(8,128)}) %all-reduce.11.cloned.1.call-update) | async-done | bytes 1572880 | tf_op jit(solution)/shard_map/psum | solution.py:29
  415.4 2.4 fusion.14
  (63 shorter events, 18.2 us)
Async XLA Ops:
  7.2 9.6 %copy-start.11 = (s32[4]{0:T(128)S(1)}, s32[4]{0:T(128)}, u32[]{:S(2)}) copy-start(s32[4]{0:T(128)} %param.13) | copy-start | bytes 52
  7.2 10.2 %copy-start.12 = (s32[4]{0:T(128)S(1)}, s32[4]{0:T(128)}, u32[]{:S(2)}) copy-start(s32[4]{0:T(128)} %param.12) | copy-start | bytes 52
  7.2 63.9 %copy-start.7 = (s32[2048]{0:T(1024)S(1)}, s32[2048]{0:T(1024)}, u32[]{:S(2)}) copy-start(s32[2048]{0:T(1024)} %param.15) | copy-start | bytes 24580
  7.2 63.8 %copy-start.6 = (f32[4,168,32]{1,2,0:T(8,128)S(1)}, f32[4,168,32]{1,2,0:T(8,128)}, u32[]{:S(2)}) copy-start(f32[4,168,32]{1,2,0:T(8,128)} %param.19) | copy-start | bytes 258052
  7.2 97.3 %all-reduce.5.cloned.1.call-start = ((), (), s32[]{:S(2)}) async-start(), calls=%async_computation | async-start | bytes 393216 | tf_op jit(solution)/shard_map/psum | solution.py:30
  8.8 68.0 %copy-start.9 = (f32[2048]{0:T(1024)S(1)}, f32[2048]{0:T(1024)}, u32[]{:S(2)}) copy-start(f32[2048]{0:T(1024)} %param.18) | copy-start | bytes 24580
  8.8 68.0 %copy-start.10 = (f32[2048]{0:T(1024)S(1)}, f32[2048]{0:T(1024)}, u32[]{:S(2)}) copy-start(f32[2048]{0:T(1024)} %param.17) | copy-start | bytes 24580
  12.0 184.5 %all-reduce.7.cloned.1.call-start = ((), (), s32[]{:S(2)}) async-start(), calls=%async_computation.1 | async-start | bytes 3145728 | tf_op jit(solution)/shard_map/psum | solution.py:29
  16.7 306.8 %all-reduce.9.cloned.1.call-start = ((), (), s32[]{:S(2)}) async-start(), calls=%async_computation.2 | async-start | bytes 393216 | tf_op jit(solution)/shard_map/psum | solution.py:30
  71.0 5.7 %copy-start = (f32[4,168,2048]{2,1,0:T(8,128)S(1)}, f32[4,168,2048]{2,1,0:T(8,128)}, u32[]{:S(2)}) copy-start(f32[4,168,2048]{2,1,0:T(8,128)} %param.10) | copy-start | bytes 16515076
  79.8 2.4 copy-start.1
  82.2 117.4 %copy-start.5 = (f32[4,48,2048]{2,1,0:T(8,128)S(1)}, f32[4,48,2048]{2,1,0:T(8,128)}, u32[]{:S(2)}) copy-start(f32[4,48,2048]{2,1,0:T(8,128)} %param.11) | copy-start | bytes 4718596
  196.5 3.1 copy-start.2
  199.5 3.0 slice-start
  199.5 3.8 slice-start.4
  199.5 3.8 copy-start.8
  199.6 4.4 %slice-start.1 = ((s8[5505024]{0:T(1024)(128)(4,1)}), s8[1310720]{0:T(1024)(128)(4,1)S(1)}, s32[]{:S(2)}) async-start(s8[5505024]{0:T(1024)(128)(4,1)} %bitcast.41), calls=%async_computation.5 | async-start | bytes 2621440
  202.5 23.1 %copy-start.3 = (f32[4,48,2048]{2,1,0:T(8,128)}, f32[4,48,2048]{2,1,0:T(8,128)S(1)}, u32[]{:S(2)}) copy-start(f32[4,48,2048]{2,1,0:T(8,128)S(1)} %get-tuple-element.9) | copy-start | bytes 4718596
  214.0 2.2 slice-start.2
  214.5 2.2 slice-start.3
  229.1 2.4 copy-start.4
  234.3 181.1 %all-reduce.11.cloned.1.call-start = ((), (), s32[]{:S(2)}) async-start(), calls=%async_computation.3 | async-start | bytes 3145728 | tf_op jit(solution)/shard_map/psum | solution.py:29
Sparse Core Ops, SparseCore 0:
  12.1 92.3 all-reduce.4
  108.6 87.8 all-reduce.6
  234.4 89.0 all-reduce.8
  327.5 87.8 all-reduce.10
where the time goes:
time: 429 us; the launch traced here: 428 us
  waiting for transfers between devices  255 us (59%)
  blocking collectives  86.1 us (20%)
  matrix products  37.2 us (9%)
  other arithmetic  18.6 us (4%)
  between operations  16.5 us (4%)
  local copies, waits for them, and re-layouts  14.7 us (3%)
    psum x2, waiting for transfers between devices, average(): day_two, node_weight = lax.psum((day_two, node_weight), 'sub')  181 us
    psum x2, waiting for transfers between devices, average(): lax.psum((day_one, weight_sum, riding), ('branch', 'sub'))  74.3 us
    psum x1, blocking collectives, average(): lax.psum((day_one, weight_sum, riding), ('branch', 'sub'))  35.9 us
    psum x1, blocking collectives, shards(): dev_total = lax.psum(local_spread, ('branch', 'sub'))  32.6 us
    psum x1, blocking collectives, average(): day_two, node_weight = lax.psum((day_two, node_weight), 'sub')  17.6 us
    dot_general x3, matrix products, shards(): jnp.einsum('stg,gz->stz', current, zone_table, precision=lax.Precision.HI...  11.6 us
    min x3, other arithmetic, shards(): current = jnp.clip(current - step_size * gradient, 0.0, ceiling)  9.51 us
    unnamed x35, local copies, waits for them, and re-layouts  9.42 us
  transfers between devices with their start and end apart: 4, of which 4 were waited for; matrix products, arithmetic and copies ran while one was open for 5% of the time, Pallas kernels for 0%

commit v1 on v0

--- a/solution.py
+++ b/solution.py
@@ -27,7 +27,9 @@
     )
     node_weight = jnp.sum(weighted, axis=1)
     day_two, node_weight = lax.psum((day_two, node_weight), "sub")
-    day_one, weight_sum, riding = lax.psum((day_one, weight_sum, riding), ("branch", "sub"))
+    day_one, weight_sum, riding = lax.psum(
+        lax.psum((day_one, weight_sum, riding), "sub"), axis_name="branch"
+    )
     root_mean = day_one / weight_sum[0]
     node_mean = day_two / node_weight[:, None, None]
     assigned = jnp.einsum("ks,ktg->stg", member, node_mean, precision=lax.Precision.HIGHEST)

time: 429 us -> 302 us (0.70)
  waiting for transfers between devices: 255 us -> 147 us
  blocking collectives: 86.1 us -> 63.8 us
    psum x2, waiting for transfers between devices: 181 us -> 113 us  [average(): day_two, node_weight = lax.psum((day_two, node_weight), 'sub')]
    psum x2, waiting for transfers between devices: 74.3 us -> 33.6 us  [average(): lax.psum(lax.psum((day_one, weight_sum, riding), 'sub'), axis_name='branch')]
    psum x1, blocking collectives: 35.9 us -> 3.13 us  [average(): lax.psum(lax.psum((day_one, weight_sum, riding), 'sub'), axis_name='branch')]
    psum x1, blocking collectives: 17.6 us -> 24.7 us  [average(): day_two, node_weight = lax.psum((day_two, node_weight), 'sub')]
    unnamed x35 -> x31, local copies, waits for them, and re-layouts: 9.42 us -> 9.04 us
  transfers between devices with their start and end apart: 4 -> 4, of which waited for: 4 -> 4; matrix products, arithmetic and copies ran while one was open for 5% -> 6% of each run, Pallas kernels for 0% -> 0%
where the time goes in v1:
time: 302 us
  waiting for transfers between devices  147 us (49%)
  blocking collectives  63.8 us (21%)
  matrix products  39.5 us (13%)
  other arithmetic  20.3 us (7%)
  between operations  16.5 us (5%)
  local copies, waits for them, and re-layouts  14.4 us (5%)
    psum x2, waiting for transfers between devices, average(): day_two, node_weight = lax.psum((day_two, node_weight), 'sub')  113 us
    psum x1, blocking collectives, shards(): dev_total = lax.psum(local_spread, ('branch', 'sub'))  36 us
    psum x2, waiting for transfers between devices, average(): lax.psum(lax.psum((day_one, weight_sum, riding), 'sub'), axis_name='branch')  33.6 us
    psum x1, blocking collectives, average(): day_two, node_weight = lax.psum((day_two, node_weight), 'sub')  24.7 us
    dot_general x3, matrix products, shards(): jnp.einsum('stg,gz->stz', current, zone_table, precision=lax.Precision.HI...  11.5 us
    dot_general x3, matrix products, shards(): jnp.einsum('stz,gz->stg', mismatch, zone_table, precision=lax.Precision.H...  11.5 us
    min x3, other arithmetic, shards(): current = jnp.clip(current - step_size * gradient, 0.0, ceiling)  9.8 us
    unnamed x31, local copies, waits for them, and re-layouts  9.04 us
  transfers between devices with their start and end apart: 4, of which 4 were waited for; matrix products, arithmetic and copies ran while one was open for 6% of the time, Pallas kernels for 0%

profile of v1, /device:TPU:0, one launch (start us, length us, event | category | flops | bytes accessed | tf_op | source)
XLA Modules:
  0.0 301.8 jit_solution(16410130114054210034)
XLA Ops:
  9.4 2.5 fusion.25
  12.6 4.0 %fusion.23 = f32[8,24,2048]{2,0,1:T(8,128)} fusion(f32[4,24,2048]{2,1,0:T(8,128)S(1)} %get-tuple-element.20, f32[4]{0:T(128)S(1)} %convert_element_type.5, s32[4]{0:T(128)} %param.12), kind=kOutput, calls=%fused_computation.41 | convolution fusion | flops 18874432 | bytes 2359328 | tf_op jit(solution)/shard_map/ks,stg->ktg/dot_general | solution.py:25
  17.4 24.7 %all-reduce = (f32[8]{0:T(128)S(1)}, f32[1]{0:T(128)}) all-reduce(f32[8]{0:T(128)S(1)} %select_reduce_fusion, f32[1]{0:T(128)} %bitcast.4), channel_id=1, replica_groups=mesh['groups'=2,'branch'=2,'sub'=8] {'sub'}, use_global_device_ids=true, to_apply=%region_7.0 | all-reduce | flops 9 | bytes 72 | tf_op jit(solution)/shard_map/psum | solution.py:29
  42.1 3.1 %psum.82 = f32[1]{0:T(128)} all-reduce(f32[1]{0:T(128)} %get-tuple-element.9), channel_id=1, replica_groups=mesh['groups'=2,'branch'=2,'sub'=8] {'branch'}, use_global_device_ids=true, to_apply=%region_4.0 | all-reduce | flops 1 | bytes 8 | tf_op jit(solution)/shard_map/psum | solution.py:30
  45.2 5.6 %fusion.18 = f32[4,168,32]{1,2,0:T(8,128)S(1)} fusion(f32[4,168,32]{1,2,0:T(8,128)S(1)} %copy-done.4, f32[4,168,2048]{2,1,0:T(8,128)} %param.10, s32[2048]{0:T(1024)S(1)} %copy-done.5), kind=kOutput, calls=%fused_computation.36 | convolution fusion | flops 528569344 | bytes 5685248 | tf_op jit(solution)/shard_map/stg,gz->stz/dot_general | solution.py:71
  50.8 5.6 %multiply_add_fusion.2 = f32[4,168,2048]{2,1,0:T(8,128)S(1)} fusion(f32[4,168,2048]{2,1,0:T(8,128)} %param.10, f32[4,168,32]{1,2,0:T(8,128)S(1)} %fusion.18, f32[2048]{0:T(1024)S(1)} %copy-done.7, f32[2048]{0:T(1024)S(1)} %copy-done.8, s32[2048]{0:T(1024)S(1)} %copy-done.5), kind=kOutput, calls=%fused_computation.14 | convolution fusion | flops 534052864 | bytes 11120640 | tf_op jit(solution)/shard_map/stz,gz->stg/dot_general | solution.py:73
  56.4 2.4 copy-done
  58.8 54.9 %all-reduce.14.cloned.1.call-done = (f32[8,24,2048]{2,0,1:T(8,128)}, f32[24,2048]{1,0:T(8,128)}) async-done(((f32[8,24,2048]{2,0,1:T(8,128)}, f32[24,2048]{1,0:T(8,128)}), (f32[8,24,2048]{2,0,1:T(8,128)}, f32[24,2048]{1,0:T(8,128)})) %all-reduce.14.cloned.1.call-update) | async-done | bytes 1769488 | tf_op jit(solution)/shard_map/psum | solution.py:29
  114.0 2.4 fusion.16
  117.7 16.1 %all-reduce.8.cloned.1.call-done = f32[24,2048]{1,0:T(8,128)} async-done(((f32[24,2048]{1,0:T(8,128)}), f32[24,2048]{1,0:T(8,128)}) %all-reduce.8.cloned.1.call-update) | async-done | bytes 196624 | tf_op jit(solution)/shard_map/psum | solution.py:30
  135.8 4.1 %fusion.12 = (f32[4,48,2048]{2,1,0:T(8,128)S(1)}, f32[4,48,2048]{2,1,0:T(8,128)S(1)}, f32[]{:T(128)}) fusion(f32[4,168,2048]{2,1,0:T(8,128)} %copy-done, f32[4,24,2048]{2,1,0:T(8,128)} %copy.14, f32[4,24,2048]{2,1,0:T(8,128)S(1)} %broadcast_in_dim.9, f32[4,168,2048]{2,1,0:T(8,128)} %param.10, f32[4,48,2048]{2,1,0:T(8,128)} %param.11, ...), kind=kLoop, calls=%fused_computation.25 | loop fusion | flops 3145727 | bytes 9437204 | tf_op jit(solution)/shard_map/add | solution.py:76
  139.9 4.3 %fusion.2 = f32[4,168,2048]{2,1,0:T(8,128)S(1)} fusion(f32[4,168,2048]{2,1,0:T(8,128)S(1)} %bitcast.42, f32[4,120,2048]{2,1,0:T(8,128)S(1)} %slice-done.4, f32[4,48,2048]{2,1,0:T(8,128)S(1)} %get-tuple-element.14, s32[4,168,2048]{2,1,0:T(8,128)} %param.14, f32[2048]{0:T(1024)S(1)} %copy-done.6), kind=kLoop, calls=%fused_computation.3 | loop fusion | flops 9633792 | bytes 22028288 | tf_op jit(solution)/shard_map/jit(clip)/min | solution.py:81
  144.2 3.0 convolution_subtract_fusion.1
  147.2 3.0 multiply_add_fusion.1
  153.1 2.8 fusion.5
  156.0 3.0 convolution_subtract_fusion
  159.0 3.0 multiply_add_fusion
  163.0 2.6 fusion.8
  165.6 2.4 copy-done.3
  170.8 3.3 %fusion.19 = f32[8,24,2048]{2,0,1:T(8,128)} fusion(f32[4,24,2048]{2,1,0:T(8,128)S(1)} %get-tuple-element.18, f32[4]{0:T(128)S(1)} %convert_element_type.5, s32[4]{0:T(128)S(1)} %copy-done.10), kind=kOutput, calls=%fused_computation.37 | convolution fusion | flops 18874432 | bytes 2359328 | tf_op jit(solution)/shard_map/ks,stg->ktg/dot_general | solution.py:25
  174.8 36.0 %psum.88 = f32[1]{0:T(128)} all-reduce(f32[1]{0:T(128)} %bitcast.10), channel_id=1, replica_groups=mesh['groups'=2,'branch'=2,'sub'=8] {'branch','sub'}, use_global_device_ids=true, to_apply=%region_12.13 | all-reduce | flops 1 | bytes 8 | tf_op jit(solution)/shard_map/psum | solution.py:62
  211.5 58.4 %all-reduce.12.cloned.1.call-done = (f32[8,24,2048]{2,0,1:T(8,128)}, f32[24,2048]{1,0:T(8,128)}) async-done(((f32[8,24,2048]{2,0,1:T(8,128)}, f32[24,2048]{1,0:T(8,128)}), (f32[8,24,2048]{2,0,1:T(8,128)}, f32[24,2048]{1,0:T(8,128)})) %all-reduce.12.cloned.1.call-update) | async-done | bytes 1769488 | tf_op jit(solution)/shard_map/psum | solution.py:29
  269.9 2.4 fusion.14
  272.3 17.4 %all-reduce.10.cloned.1.call-done = f32[24,2048]{1,0:T(8,128)} async-done(((f32[24,2048]{1,0:T(8,128)}), f32[24,2048]{1,0:T(8,128)}) %all-reduce.10.cloned.1.call-update) | async-done | bytes 196624 | tf_op jit(solution)/shard_map/psum | solution.py:30
  (59 shorter events, 18.2 us)
Async XLA Ops:
  7.2 9.6 %copy-start.9 = (s32[4]{0:T(128)S(1)}, s32[4]{0:T(128)}, u32[]{:S(2)}) copy-start(s32[4]{0:T(128)} %param.13) | copy-start | bytes 52
  7.2 10.2 %copy-start.10 = (s32[4]{0:T(128)S(1)}, s32[4]{0:T(128)}, u32[]{:S(2)}) copy-start(s32[4]{0:T(128)} %param.12) | copy-start | bytes 52
  7.2 38.0 %copy-start.5 = (s32[2048]{0:T(1024)S(1)}, s32[2048]{0:T(1024)}, u32[]{:S(2)}) copy-start(s32[2048]{0:T(1024)} %param.15) | copy-start | bytes 24580
  7.2 38.0 %copy-start.4 = (f32[4,168,32]{1,2,0:T(8,128)S(1)}, f32[4,168,32]{1,2,0:T(8,128)}, u32[]{:S(2)}) copy-start(f32[4,168,32]{1,2,0:T(8,128)} %param.19) | copy-start | bytes 258052
  7.2 106.5 %all-reduce.14.cloned.1.call-start = ((), (), s32[]{:S(2)}) async-start(), calls=%async_computation.3 | async-start | bytes 3538944 | tf_op jit(solution)/shard_map/psum | solution.py:29
  9.4 41.4 %copy-start.7 = (f32[2048]{0:T(1024)S(1)}, f32[2048]{0:T(1024)}, u32[]{:S(2)}) copy-start(f32[2048]{0:T(1024)} %param.18) | copy-start | bytes 24580
  9.4 41.4 %copy-start.8 = (f32[2048]{0:T(1024)S(1)}, f32[2048]{0:T(1024)}, u32[]{:S(2)}) copy-start(f32[2048]{0:T(1024)} %param.17) | copy-start | bytes 24580
  16.7 117.1 %all-reduce.8.cloned.1.call-start = ((), (), s32[]{:S(2)}) async-start(), calls=%async_computation | async-start | bytes 393216 | tf_op jit(solution)/shard_map/psum | solution.py:30
  56.4 2.4 copy-start
  113.8 156.1 %all-reduce.12.cloned.1.call-start = ((), (), s32[]{:S(2)}) async-start(), calls=%async_computation.2 | async-start | bytes 3538944 | tf_op jit(solution)/shard_map/psum | solution.py:29
  117.7 22.2 %slice-start = ((s8[5505024]{0:T(1024)(128)(4,1)}), s8[1310720]{0:T(1024)(128)(4,1)S(1)}, s32[]{:S(2)}) async-start(s8[5505024]{0:T(1024)(128)(4,1)} %bitcast.41), calls=%async_computation.4 | async-start | bytes 2621440
  117.7 22.2 %copy-start.6 = (f32[2048]{0:T(1024)S(1)}, f32[2048]{0:T(1024)}, u32[]{:S(2)}) copy-start(f32[2048]{0:T(1024)} %param.16) | copy-start | bytes 24580
  133.8 6.1 %slice-start.4 = ((f32[4,168,2048]{2,1,0:T(8,128)}), f32[4,120,2048]{2,1,0:T(8,128)S(1)}, s32[]{:S(2)}) async-start(f32[4,168,2048]{2,1,0:T(8,128)} %copy-done), calls=%async_computation.8 | async-start | bytes 7864320 | tf_op jit(solution)/shard_map/slice | solution.py:80
  135.8 4.1 %slice-start.1 = ((s8[5505024]{0:T(1024)(128)(4,1)}), s8[4194304]{0:T(1024)(128)(4,1)S(1)}, s32[]{:S(2)}) async-start(s8[5505024]{0:T(1024)(128)(4,1)} %bitcast.41), calls=%async_computation.5 | async-start | bytes 8388608
  139.9 22.1 %copy-start.1 = (f32[4,48,2048]{2,1,0:T(8,128)}, f32[4,48,2048]{2,1,0:T(8,128)S(1)}, u32[]{:S(2)}) copy-start(f32[4,48,2048]{2,1,0:T(8,128)S(1)} %get-tuple-element.15) | copy-start | bytes 4718596
  150.2 1.1 copy-start.2
  150.3 2.4 slice-start.2
  150.5 2.6 slice-start.3
  165.6 2.4 copy-start.3
  174.2 115.6 %all-reduce.10.cloned.1.call-start = ((), (), s32[]{:S(2)}) async-start(), calls=%async_computation.1 | async-start | bytes 393216 | tf_op jit(solution)/shard_map/psum | solution.py:30
Sparse Core Ops, SparseCore 0:
  16.8 96.9 all-reduce.13
  116.2 17.5 all-reduce.7
  174.3 95.5 all-reduce.11
  272.1 17.6 all-reduce.9
